TPU v7x, 128 devices: a whole 4x4x4 slice. The times are simulated.
128 devices in a mesh: gy: 32 (over z, y, core), var: 4 (over x).
Axes of the slice: x: 4, y: 4, z: 4, core: 2. Of those that a mesh axis runs over, the one named last changes fastest.
Arguments:
- field: float32 [32, 32, 1024, 128], P('var', None, 'gy')
- factor_x: float32 [32, 16], replicated, may hold values from -1 to 1
- factor_y: float32 [1024, 64], P('gy'), may hold values from -0.1875 to 0.1875
- factor_z: float32 [128, 64], replicated, may hold values from -0.5 to 0.5
- factor_v: float32 [32, 16], replicated, may hold values from -1 to 1
Outputs:
- proj_z: float32 [128, 128], replicated
- proj_v: float32 [32, 32], replicated
- core_rms: float32 [], replicated
All inputs are finite; a program needn't handle non-finite values.
Results may differ from a plain program's by a relative error of at most 0.0003.
Values sent between devices are 32-bit elements; how exact they have to be, the bound alone decides.
No kernel may reach another device: no remote copies, remote signals or barrier semaphores. Data moves between devices by JAX's collectives and lax.ppermute only.
A program may use at most 192 MiB of HBM per device.

v0:
```python
import jax
import jax.numpy as jnp
from jax import lax
from jax.sharding import PartitionSpec as P

precise = lax.Precision.HIGHEST


def orth(mat):
    gram = jnp.dot(mat.T, mat, precision=precise)
    lower = jnp.linalg.cholesky(gram)
    return jax.scipy.linalg.solve_triangular(lower, mat.T, lower=True).T


def total_core(local_part):
    return lax.psum(local_part, ("gy", "var"))


def per_device(field, factor_x, factor_y, factor_z, factor_v):
    var_rows = field.shape[0]
    var_start = lax.axis_index("var") * var_rows
    local_v = lax.dynamic_slice_in_dim(factor_v, var_start, var_rows, 0)
    along_x = jnp.einsum("vxyz,xa->vayz", field, factor_x, precision=precise)
    partial_value = jnp.einsum("vayz,yb->vabz", along_x, factor_y, precision=precise)
    wide_z = jnp.einsum("vabz,vc->cabz", partial_value, local_v, precision=precise)
    fibres = lax.psum_scatter(wide_z, ("gy", "var"), scatter_dimension=3, tiled=True)
    z_count = fibres.shape[3]
    z_start = lax.axis_index(("gy", "var")) * z_count
    local_z = lax.dynamic_slice_in_dim(factor_z, z_start, z_count, 0)
    small_core = total_core(jnp.einsum("cabz,zr->cabr", fibres, local_z, precision=precise))
    rows_z = jnp.einsum("cabz,cabr->zr", fibres, small_core, precision=precise)
    raw_z = lax.all_gather(rows_z, ("gy", "var"), axis=0, tiled=True)
    new_z = orth(raw_z)
    proj_z = jnp.dot(new_z, new_z.T, precision=precise)
    wide_v = jnp.einsum("vabz,zr->vabr", partial_value, new_z, precision=precise)
    flat_v = wide_v.reshape(var_rows, -1)
    summed_v = lax.psum(flat_v, "gy")
    every_v = lax.all_gather(summed_v, "var", axis=0, tiled=True)
    gram_v = jnp.dot(every_v, every_v.T, precision=precise)
    new_v = orth(jnp.dot(gram_v, factor_v, precision=precise))
    proj_v = jnp.dot(new_v, new_v.T, precision=precise)
    core = jnp.dot(new_v.T, every_v, precision=precise)
    core_rms = jnp.sqrt(jnp.mean(core * core))
    return (proj_z, proj_v, core_rms)


def solution(mesh):
    in_specs = (P("var", None, "gy", None), P(), P("gy", None), P(), P())
    out_specs = (P(), P(), P())
    return jax.shard_map(
        per_device, mesh=mesh, in_specs=in_specs, out_specs=out_specs, check_vma=False
    )
```

profile of v0, /device:TPU:1, one launch (start us, length us, event | category | flops | bytes accessed | tf_op | source)
XLA Modules:
  0.0 1346.6 jit_solution(12369558590492828368)
XLA Ops:
  7.2 6.9 fusion.5
  14.1 4.1 convolution_bitcast_fusion
  18.2 2.0 copy-done.1
  20.2 5.2 copy.21
  25.4 122.6 %fusion.25 = f32[16,131072]{0,1} fusion(f32[8,131072]{1,0:T(8,128)} %bitcast.65, f32[32,16]{0,1:T(8,128)S(1)} %copy-done.3, s32[]{:T(128)S(6)} %select_n.14), kind=kOutput, calls=%fused_computation.35 | convolution fusion | flops 201326592 | bytes 71305216
  148.0 42.6 %copy.22 = f32[16,16,64,128]{2,1,0,3:T(8,128)} copy(f32[16,16,64,128]{0,3,2,1:T(8,128)} %bitcast.7) | data formatting | bytes 16777216 | tf_op jit(solution)/shard_map/vabz,vc->cabz/dot_general | solution.py:25
  190.8 0.2 dynamic-slice_reduce_fusion
  190.9 668.2 %reduce-scatter.2.cloned.1.call-done = f32[16,16,64,1]{2,1,0,3:T(8,128)} async-done(((f32[16,16,64,128]{2,1,0,3:T(8,128)}), f32[16,16,64,1]{2,1,0,3:T(8,128)}) %reduce-scatter.2.cloned.1.call-update) | async-done | bytes 65552 | tf_op jit(solution)/shard_map/reduce_scatter | solution.py:26
  859.1 5.5 broadcast_multiply_fusion
  864.7 165.4 %all-reduce.4.cloned.1.call-done = f32[16,16,64,64]{3,2,1,0:T(8,128)} async-done(((f32[16,16,64,64]{3,2,1,0:T(8,128)}), f32[16,16,64,64]{3,2,1,0:T(8,128)}) %all-reduce.4.cloned.1.call-update) | async-done | bytes 4194320 | tf_op jit(solution)/shard_map/psum | solution.py:16
  1030.1 6.6 fusion.9
  1036.8 0.3 dynamic-update-slice.6
  1037.0 64.0 %all-reduce = f32[8192]{0:T(1024)S(1)} all-reduce(f32[8192]{0:T(1024)S(1)} %dynamic-update-slice.6), channel_id=2, replica_groups=mesh['gy'=32,'var'=4] {'gy','var'}, use_global_device_ids=true, to_apply=%add | all-reduce | flops 8192 | bytes 65536
  1101.2 0.3 fusion.28
  1101.5 5.8 cholesky.29
  1107.4 0.6 compare_reduce_fusion.1
  1108.0 0.7 fusion.13
  1108.7 4.9 custom-call.14
  1113.6 0.3 fusion.16
  1113.9 6.6 fusion.14
  1120.5 4.7 reshape.38
  1125.3 104.6 %all-reduce.6.cloned.1.call-done = f32[8,65536]{1,0:T(8,128)} async-done(((f32[8,65536]{1,0:T(8,128)}), f32[8,65536]{1,0:T(8,128)}) %all-reduce.6.cloned.1.call-update) | async-done | bytes 2097168 | tf_op jit(solution)/shard_map/psum | solution.py:37
  1229.9 0.9 fusion.29
  1230.8 83.4 %all-gather.3.cloned.1.call-done = f32[32,65536]{1,0:T(8,128)} async-done(((f32[8,65536]{1,0:T(8,128)}), f32[32,65536]{1,0:T(8,128)}) %all-gather.3.cloned.1.call-update) | async-done | bytes 8388624 | tf_op jit(solution)/shard_map/all_gather | solution.py:38
  1314.2 10.7 fusion.30
  1325.2 1.5 cholesky.61
  1326.7 0.6 compare_reduce_fusion
  1327.4 0.6 fusion.20
  1328.0 1.2 custom-call.15
  1329.3 0.2 fusion.22
  1329.5 0.8 fusion.33
  1330.3 7.5 fusion.8
  (27 shorter events, 0.8 us)
Async XLA Ops:
  7.2 183.6 %copy-start = (f32[128,64]{0,1:T(8,128)S(1)}, f32[128,64]{0,1:T(8,128)}, u32[]{:S(2)}) copy-start(f32[128,64]{0,1:T(8,128)} %param.8) | copy-start | bytes 98308
  7.2 6.9 copy-start.4
  7.2 851.9 %reduce-scatter.2.cloned.1.call-start = ((), (), s32[]{:S(2)}) async-start(), calls=%async_computation.1 | async-start | bytes 16908288 | tf_op jit(solution)/shard_map/reduce_scatter | solution.py:26
  18.2 2.0 copy-start.1
  20.2 5.3 copy-start.3
  190.7 839.4 %all-reduce.4.cloned.1.call-start = ((), (), s32[]{:S(2)}) async-start(), calls=%async_computation.2 | async-start | bytes 16777216 | tf_op jit(solution)/shard_map/psum | solution.py:16
  864.6 165.5 %copy-start.2 = (f32[16,16,64,1]{2,1,0,3:T(8,128)S(1)}, f32[16,16,64,1]{2,1,0,3:T(8,128)}, u32[]{:S(2)}) copy-start(f32[16,16,64,1]{2,1,0,3:T(8,128)} %reduce-scatter.2.cloned.1.call-done) | copy-start | bytes 196612
  864.6 365.3 %all-reduce.6.cloned.1.call-start = ((), (), s32[]{:S(2)}) async-start(), calls=%async_computation.3 | async-start | bytes 4194304 | tf_op jit(solution)/shard_map/psum | solution.py:37
  1125.2 189.0 %all-gather.3.cloned.1.call-start = ((), (), s32[]{:S(2)}) async-start(), calls=%async_computation.4 | async-start | bytes 10485760 | tf_op jit(solution)/shard_map/all_gather | solution.py:38
Sparse Core Ops, SparseCore 0:
  190.8 668.2 reduce-scatter.1
  864.7 165.3 all-reduce.3
  1125.3 104.5 all-reduce.5
  1231.5 82.6 all-gather.2
where the time goes:
time: 1350 us
  waiting for transfers between devices  1020 us (76%)
  matrix products  168 us (12%)
  blocking collectives  64 us (5%)
  local copies, waits for them, and re-layouts  55.3 us (4%)
  other arithmetic  21.6 us (2%)
  between operations  16.2 us (1%)
    reduce_scatter x1, waiting for transfers between devices, per_device(): lax.psum_scatter(wide_z, ('gy', 'var'), scatter_dimension=3, tiled=True)  668 us
    psum x1, waiting for transfers between devices, total_core(): return lax.psum(local_part, ('gy', 'var'))  165 us
    unnamed x1, matrix products  123 us
    psum x1, waiting for transfers between devices, per_device(): summed_v = lax.psum(flat_v, 'gy')  105 us
    all_gather x1, waiting for transfers between devices, per_device(): every_v = lax.all_gather(summed_v, 'var', axis=0, tiled=True)  83.4 us
    unnamed x1, blocking collectives  64 us
    dot_general x1, local copies, waits for them, and re-layouts, per_device(): jnp.einsum('vabz,vc->cabz', partial_value, local_v, precision=precise)  42.6 us
  transfers between devices with their start and end apart: 4, of which 4 were waited for; matrix products, arithmetic and copies ran while one was open for 0% of the time, Pallas kernels for 0%

commit v1 on v0

--- a/solution.py
+++ b/solution.py
@@ -35,7 +35,22 @@
     wide_v = jnp.einsum("vabz,zr->vabr", partial_value, new_z, precision=precise)
     flat_v = wide_v.reshape(var_rows, -1)
     summed_v = lax.psum(flat_v, "gy")
-    every_v = lax.all_gather(summed_v, "var", axis=0, tiled=True)
+    ways, here, step = (lax.axis_size("var"), lax.axis_index("var"), summed_v.shape[0])
+    shape = [n * ways if d == 0 else n for d, n in enumerate(summed_v.shape)]
+    every_v = lax.dynamic_update_slice_in_dim(
+        jnp.zeros(shape, summed_v.dtype), summed_v, here * step, axis=0
+    )
+    going_up = going_down = summed_v
+    for far in range(1, ways // 2 + 1):
+        going_up = lax.ppermute(going_up, "var", [(d, (d + 1) % ways) for d in range(ways)])
+        every_v = lax.dynamic_update_slice_in_dim(
+            every_v, going_up, (here - far) % ways * step, axis=0
+        )
+        if 2 * far < ways:
+            going_down = lax.ppermute(going_down, "var", [(d, (d - 1) % ways) for d in range(ways)])
+            every_v = lax.dynamic_update_slice_in_dim(
+                every_v, going_down, (here + far) % ways * step, axis=0
+            )
     gram_v = jnp.dot(every_v, every_v.T, precision=precise)
     new_v = orth(jnp.dot(gram_v, factor_v, precision=precise))
     proj_v = jnp.dot(new_v, new_v.T, precision=precise)

time: 1350 us -> 1350 us (level)
  matrix products: 168 us -> 153 us
    ppermute x0 -> x3, waiting for transfers between devices: none -> 90.8 us  [the longest x2 90.8 us: per_device(): lax.ppermute(going_up, 'var', [(d, (d + 1) % ways) for d in range(ways)])]
    all_gather x1 -> x0, waiting for transfers between devices: 83.4 us -> none  [per_device(): every_v = lax.all_gather(summed_v, 'var', axis=0, tiled=True)]
  transfers between devices with their start and end apart: 4 -> 6, of which waited for: 4 -> 5; matrix products, arithmetic and copies ran while one was open for 0% -> 0% of each run, Pallas kernels for 0% -> 0%
where the time goes in v1:
time: 1350 us; the launch traced here: 1340 us
  waiting for transfers between devices  1030 us (76%)
  matrix products  153 us (11%)
  blocking collectives  64.1 us (5%)
  local copies, waits for them, and re-layouts  56.6 us (4%)
  other arithmetic  21.7 us (2%)
  between operations  16 us (1%)
    reduce_scatter x1, waiting for transfers between devices, per_device(): lax.psum_scatter(wide_z, ('gy', 'var'), scatter_dimension=3, tiled=True)  667 us
    psum x1, waiting for transfers between devices, total_core(): return lax.psum(local_part, ('gy', 'var'))  166 us
    unnamed x1, matrix products  111 us
    psum x1, waiting for transfers between devices, per_device(): summed_v = lax.psum(flat_v, 'gy')  104 us
    ppermute x2, waiting for transfers between devices, per_device(): lax.ppermute(going_up, 'var', [(d, (d + 1) % ways) for d in range(ways)])  90.8 us
    unnamed x1, blocking collectives  64.1 us
    dot_general x1, local copies, waits for them, and re-layouts, per_device(): jnp.einsum('vabz,vc->cabz', partial_value, local_v, precision=precise)  42.7 us
  transfers between devices with their start and end apart: 6, of which 5 were waited for; matrix products, arithmetic and copies ran while one was open for 0% of the time, Pallas kernels for 0%

profile of v1, /device:TPU:1, one launch (start us, length us, event | category | flops | bytes accessed | tf_op | source)
XLA Modules:
  0.0 1342.2 jit_solution(9474778738446365874)
XLA Ops:
  7.2 6.9 fusion.5
  14.1 4.8 convolution_bitcast_fusion
  18.9 2.0 copy-done.2
  20.9 5.2 copy.21
  26.2 111.2 %fusion.25 = f32[16,131072]{0,1} fusion(f32[8,131072]{1,0:T(8,128)} %bitcast.65, f32[32,16]{0,1:T(8,128)S(1)} %copy-done.5, s32[]{:T(128)S(6)} %select_n.39), kind=kOutput, calls=%fused_computation.35 | convolution fusion | flops 201326592 | bytes 71305216
  137.3 42.7 %copy.22 = f32[16,16,64,128]{2,1,0,3:T(8,128)} copy(f32[16,16,64,128]{0,3,2,1:T(8,128)} %bitcast.7) | data formatting | bytes 16777216 | tf_op jit(solution)/shard_map/vabz,vc->cabz/dot_general | solution.py:25
  180.3 667.3 %reduce-scatter.2.cloned.1.call-done = f32[16,16,64,1]{2,1,0,3:T(8,128)} async-done(((f32[16,16,64,128]{2,1,0,3:T(8,128)}), f32[16,16,64,1]{2,1,0,3:T(8,128)}) %reduce-scatter.2.cloned.1.call-update) | async-done | bytes 65552 | tf_op jit(solution)/shard_map/reduce_scatter | solution.py:26
  847.5 5.5 broadcast_multiply_fusion
  853.2 166.2 %all-reduce.4.cloned.1.call-done = f32[16,16,64,64]{3,2,1,0:T(8,128)} async-done(((f32[16,16,64,64]{3,2,1,0:T(8,128)}), f32[16,16,64,64]{3,2,1,0:T(8,128)}) %all-reduce.4.cloned.1.call-update) | async-done | bytes 4194320 | tf_op jit(solution)/shard_map/psum | solution.py:16
  1019.3 6.6 fusion.9
  1026.2 64.1 %all-reduce = f32[8192]{0:T(1024)S(1)} all-reduce(f32[8192]{0:T(1024)S(1)} %dynamic-update-slice.6), channel_id=2, replica_groups=mesh['gy'=32,'var'=4] {'gy','var'}, use_global_device_ids=true, to_apply=%add | all-reduce | flops 8192 | bytes 65536
  1090.7 5.8 cholesky.29
  1096.6 0.6 compare_reduce_fusion.1
  1097.3 0.7 fusion.13
  1097.9 4.9 custom-call.14
  1102.8 0.3 fusion.16
  1103.1 6.6 fusion.14
  1109.7 4.7 reshape.38
  1114.5 0.9 fusion.29
  1115.4 103.7 %all-reduce.6.cloned.1.call-done = f32[8,65536]{1,0:T(8,128)} async-done(((f32[8,65536]{1,0:T(8,128)}), f32[8,65536]{1,0:T(8,128)}) %all-reduce.6.cloned.1.call-update) | async-done | bytes 2097168 | tf_op jit(solution)/shard_map/psum | solution.py:37
  1219.2 1.2 collective-permute-start
  1220.3 1.6 collective-permute-start.1
  1222.0 0.5 broadcast_in_dim.7
  1222.7 44.4 %collective-permute-done = f32[8,65536]{1,0:T(8,128)S(1)} collective-permute-done((f32[8,65536]{1,0:T(8,128)}, f32[8,65536]{1,0:T(8,128)S(1)}, u32[]{:S(2)}, u32[]{:S(2)}) %collective-permute-start) | collective-permute-done | bytes 2097184 | tf_op jit(solution)/shard_map/ppermute | solution.py:45
  1267.5 46.4 %collective-permute-done.2 = f32[8,65536]{1,0:T(8,128)S(1)} collective-permute-done((f32[8,65536]{1,0:T(8,128)S(1)}, f32[8,65536]{1,0:T(8,128)S(1)}, u32[]{:S(2)}, u32[]{:S(2)}) %collective-permute-start.2) | collective-permute-done | bytes 2097184 | tf_op jit(solution)/shard_map/ppermute | solution.py:45
  1314.1 6.6 fusion.30
  1321.1 1.5 cholesky.61
  1322.6 0.6 compare_reduce_fusion
  1323.2 0.6 fusion.20
  1323.9 1.2 custom-call.15
  1325.3 7.5 fusion.8
  1332.8 0.8 fusion.33
  (37 shorter events, 2.4 us)
Async XLA Ops:
  7.2 172.9 %copy-start = (f32[128,64]{0,1:T(8,128)S(1)}, f32[128,64]{0,1:T(8,128)}, u32[]{:S(2)}) copy-start(f32[128,64]{0,1:T(8,128)} %param.8) | copy-start | bytes 98308
  7.2 840.4 %reduce-scatter.2.cloned.1.call-start = ((), (), s32[]{:S(2)}) async-start(), calls=%async_computation.1 | async-start | bytes 16908288 | tf_op jit(solution)/shard_map/reduce_scatter | solution.py:26
  14.1 12.1 copy-start.5
  18.9 2.0 copy-start.2
  180.0 839.3 %all-reduce.4.cloned.1.call-start = ((), (), s32[]{:S(2)}) async-start(), calls=%async_computation.2 | async-start | bytes 16777216 | tf_op jit(solution)/shard_map/psum | solution.py:16
  847.5 171.8 %copy-start.4 = (f32[16,16,64,1]{2,1,0,3:T(8,128)S(1)}, f32[16,16,64,1]{2,1,0,3:T(8,128)}, u32[]{:S(2)}) copy-start(f32[16,16,64,1]{2,1,0,3:T(8,128)} %reduce-scatter.2.cloned.1.call-done) | copy-start | bytes 196612
  853.1 366.1 %all-reduce.6.cloned.1.call-start = ((), (), s32[]{:S(2)}) async-start(), calls=%async_computation.3 | async-start | bytes 4194304 | tf_op jit(solution)/shard_map/psum | solution.py:37
  1219.2 3.4 copy-start.3
  1219.2 47.9 %collective-permute-start = (f32[8,65536]{1,0:T(8,128)}, f32[8,65536]{1,0:T(8,128)S(1)}, u32[]{:S(2)}, u32[]{:S(2)}) collective-permute-start(f32[8,65536]{1,0:T(8,128)} %all-reduce.6.cloned.1.call-done), channel_id=1, source_target_pairs={{0,1},{1,2},{2,3},{3,0},{4,5},{5,6},{6,7},{7,4},{8,9},{9,10},{10,1... | collective-permute-start | bytes 6291464 | tf_op jit(solution)/shard_map/ppermute | solution.py:45
  1220.3 46.9 %collective-permute-start.1 = (f32[8,65536]{1,0:T(8,128)}, f32[8,65536]{1,0:T(8,128)S(1)}, u32[]{:S(2)}, u32[]{:S(2)}) collective-permute-start(f32[8,65536]{1,0:T(8,128)} %all-reduce.6.cloned.1.call-done), channel_id=1, source_target_pairs={{0,3},{1,0},{2,1},{3,2},{4,7},{5,4},{6,5},{7,6},{8,11},{9,8},{10,9... | collective-permute-start | bytes 6291464 | tf_op jit(solution)/shard_map/ppermute | solution.py:50
  1267.1 46.8 %collective-permute-start.2 = (f32[8,65536]{1,0:T(8,128)S(1)}, f32[8,65536]{1,0:T(8,128)S(1)}, u32[]{:S(2)}, u32[]{:S(2)}) collective-permute-start(f32[8,65536]{1,0:T(8,128)S(1)} %collective-permute-done), channel_id=1, source_target_pairs={{0,1},{1,2},{2,3},{3,0},{4,5},{5,6},{6,7},{7,4},{8,9},{9,10},{10,1... | collective-permute-start | bytes 6291464 | tf_op jit(solution)/shard_map/ppermute | solution.py:45
  1314.1 6.6 copy-start.1
Sparse Core Ops, SparseCore 0:
  180.1 667.3 reduce-scatter.1
  853.2 166.0 all-reduce.3
  1114.5 104.5 all-reduce.5
